TPU v7x, 512 devices: a whole 4x4x16 slice. The times are simulated.
512 devices in a mesh: slab: 128 (over y, z, core), led: 4 (over x).
Axes of the slice: x: 4, y: 4, z: 16, core: 2. Of those that a mesh axis runs over, the one named last changes fastest.
Arguments:
- spectrum: float32 [2, 2048, 2048], P(None, 'slab'), may hold values from -6 to 6
- led_rows: int32 [8], P('led'), may hold values from 256 to 768
- led_cols: int32 [8], P('led'), may hold values from 0 to 1024
- images: float32 [8, 1024, 1024], P('led', 'slab'), may hold values from 0.05 to 4
Outputs:
- updated: float32 [2, 2048, 2048], P(None, 'slab', 'led')
All inputs are finite; a program needn't handle non-finite values.
Results may differ from a plain program's by a relative error of at most 0.0065.
Values may be sent and summed in bfloat16 or wider, within the bound.
A program may use at most 64 MiB of HBM per device.

v0:
```python
import functools

import jax
import jax.numpy as jnp
import numpy as np
from jax import lax
from jax.experimental import pallas as pl
from jax.experimental.pallas import tpu as pltpu
from jax.sharding import PartitionSpec as P

NY, NZ, NC, NX = 4, 16, 2, 4
WIN = 1024
MESH = pl.DeviceIdType.MESH
F32, BF16 = jnp.float32, jnp.bfloat16


def grid_of(*sizes):
    return np.meshgrid(*[np.arange(n) for n in sizes], indexing="ij")


def rotation(angle_index, period, out_part, in_part, sign):
    angle = 2.0 * np.pi * (angle_index % period) / period
    same = np.cos(angle)
    cross = sign * np.sin(angle)
    return np.where(out_part == in_part, same, np.where(out_part == 1, cross, -cross))


def split(table):
    high = np.asarray(table, np.float32).astype(BF16)
    low = (table - high.astype(np.float64)).astype(np.float32).astype(BF16)
    return high, low


def make_tables():
    scale = 1.0 / 32.0
    y, c, po, z, pi, n2 = grid_of(NY, NC, 2, NZ, 2, 128)
    k2 = (y * NZ + z) * NC + c
    cols_fwd = scale * rotation(k2 * n2, 128, po, pi, -1).reshape(256, 256)
    z, l, yb, c, p, y2, c2, l2, p2, z2 = grid_of(NZ, 2, 2, NC, 2, NY, NC, 2, 2, NZ)
    hit = (z == z2) & (l == l2) & (p == p2) & (c == c2) & (y2 % 2 == yb)
    fold = hit.astype(np.float64).reshape(256, 512)
    l, po, p, z, l2, yb, c, pi = grid_of(2, 2, 64, NZ, 2, 2, NC, 2)
    strip = 32 * yb + 2 * z + c
    rows_fwd = (scale * rotation(strip * p, 64, po, pi, -1) * (l == l2)).reshape(256, 256)
    z, l, yb, c, po, l2, pi, p = grid_of(NZ, 2, 2, NC, 2, 2, 2, 64)
    strip = 32 * yb + 2 * z + c
    rows_inv = (scale * rotation(strip * p, 64, po, pi, 1) * (l == l2)).reshape(256, 256)
    pi, k1, i, po, q, k1o = grid_of(2, 8, 16, 2, 16, 8)
    short_fwd = (rotation(i * q, 16, po, pi, -1) * (k1 == k1o)).reshape(256, 256)
    pi, q, k1, po, k1o, i = grid_of(2, 16, 8, 2, 8, 16)
    short_inv = (rotation(i * q, 16, po, pi, 1) * (k1 == k1o)).reshape(256, 256)
    yb, c, l, p, z, z2, l2, yb2, c2, p2 = grid_of(2, NC, 2, 2, NZ, NZ, 2, 2, NC, 2)
    hit = (z == z2) & (l == l2) & (p == p2) & (c == c2) & (yb == yb2)
    swap = hit.astype(np.float64).reshape(256, 256)
    po, n2, y, c, pi, z = grid_of(2, 128, NY, NC, 2, NZ)
    k2 = (y * NZ + z) * NC + c
    cols_inv = scale * rotation(k2 * n2, 128, po, pi, 1).reshape(256, 256)
    halves = []
    for table in (cols_fwd, rows_fwd, short_fwd, short_inv, rows_inv, cols_inv):
        halves.extend(split(table))
    moves = [fold[:, :256], fold[:, 256:], swap]
    stack = np.stack(halves + [np.asarray(m, np.float32).astype(BF16) for m in moves])
    k1, n2 = grid_of(8, 128)
    angle = 2.0 * np.pi * ((k1 * n2) % WIN) / WIN
    twist_cols = np.stack([np.cos(angle), np.sin(angle)]).astype(np.float32)
    p, k1, i = grid_of(64, 8, 16)
    angle = (2.0 * np.pi * ((p * i) % WIN) / WIN).reshape(64, 128)
    twist_rows = np.stack([np.cos(angle), np.sin(angle)]).astype(np.float32)
    return stack, twist_cols, twist_rows


COLS_FWD, ROWS_FWD, SHORT_FWD, SHORT_INV, ROWS_INV, COLS_INV = range(0, 12, 2)
FOLD, SWAP = 12, 14


def fft(values, sign):
    size = len(values)
    if size == 1:
        return values
    even, odd = fft(values[0::2], sign), fft(values[1::2], sign)
    low, high = [], []
    for k in range(size // 2):
        (er, ei), (re, im) = even[k], odd[k]
        if k == 0:
            tr, ti = re, im
        elif 4 * k == size:
            tr, ti = (-im, re) if sign > 0 else (im, -re)
        else:
            a = float(np.cos(2 * np.pi * k / size))
            b = float(np.sin(2 * np.pi * k / size)) * sign
            tr, ti = a * re - b * im, a * im + b * re
        low.append((er + tr, ei + ti))
        high.append((er - tr, ei - ti))
    return low + high


def halves(value):
    high = value.astype(BF16)
    return high, (value - high.astype(F32)).astype(BF16)


def dot(left, right, right_dim=0):
    return lax.dot_general(
        left, right, (((1,), (right_dim,)), ((), ())), preferred_element_type=F32
    )


def dot_left(tables, at, value, right_dim=0):
    high, low = halves(value)
    return (
        dot(tables[at], high, right_dim)
        + dot(tables[at + 1], high, right_dim)
        + dot(tables[at], low, right_dim)
    )


def dot_right(value, tables, at):
    high, low = halves(value)
    return dot(high, tables[at]) + dot(low, tables[at]) + dot(high, tables[at + 1])


def step_kernel(
    led_rows, led_cols, spectrum, images, tables_in, twist_cols_in, twist_rows_in, out,
    spec, img, tables, twist_cols, twist_rows, grad,
    send1, recv1, send2, recv2, send3, recv3, send4, recv4, send5, recv5,
    in_sem, s1, r1, s2, r2, s3, r3, s4, r4, s5, r5,
):
    slab, led = lax.axis_index("slab"), lax.axis_index("led")
    core = lax.rem(slab, NC)
    z = lax.rem(lax.div(slab, NC), NZ)
    y = lax.div(slab, NC * NZ)
    yc = y * NC + core

    def slab_of(ny, nz, nc):
        return (ny * NZ + nz) * NC + nc

    near = [(2, 1), (2, 0), (1, 1), (3, 1), (1, 0), (3, 0), (0, 1)]
    near = [(lax.rem(y + dy, NY), lax.rem(core + dc, NC)) for dy, dc in near]
    far = [8, 7, 9, 6, 10, 5, 11, 4, 12, 3, 13, 2, 14, 1, 15]
    far = [lax.rem(z + dz, NZ) for dz in far]
    across = [lax.rem(led + dx, NX) for dx in (2, 1, 3)]

    barrier = pltpu.get_barrier_semaphore()
    for nz in far:
        pl.semaphore_signal(
            barrier, inc=1, device_id=(slab_of(y, nz, core), led), device_id_type=MESH
        )
    for ny, nc in near:
        pl.semaphore_signal(
            barrier, inc=1, device_id=(slab_of(ny, z, nc), led), device_id_type=MESH
        )
    for nx in across:
        pl.semaphore_signal(barrier, inc=1, device_id=(slab, nx), device_id_type=MESH)

    loads = [
        pltpu.make_async_copy(a, b, in_sem.at[n])
        for n, (a, b) in enumerate(
            [
                (spectrum, spec),
                (twist_cols_in, twist_cols),
                (tables_in.at[0:2], tables.at[0:2]),
                (images, img),
                (twist_rows_in, twist_rows),
                (tables_in.at[2:15], tables.at[2:15]),
            ]
        )
    ]
    for load in loads:
        load.start()

    row_at = slab * 16 + lax.broadcasted_iota(jnp.int32, (16, 128), 0)
    lane = lax.broadcasted_iota(jnp.int32, (16, 128), 1)

    def term(offset):
        return (2 * offset + 1 - WIN) * (2 * offset + 1 - WIN)

    row_terms = [term(row_at - led_rows[l]) for l in range(2)]

    def inside(l, block):
        return row_terms[l] + term(lane + (block * 128 - led_cols[l])) < WIN * WIN

    for load in loads[:3]:
        load.wait()
    pieces = []
    for l in range(2):
        values = []
        masks = [inside(l, block) for block in range(16)]
        for n1 in range(8):
            parts = []
            for part in range(2):
                first = spec[part, :, n1 * 128 : n1 * 128 + 128]
                second = spec[part, :, 1024 + n1 * 128 : 1152 + n1 * 128]
                parts.append(
                    jnp.where(masks[n1], first, 0.0) + jnp.where(masks[n1 + 8], second, 0.0)
                )
            values.append(tuple(parts))
        for k1, (re, im) in enumerate(fft(values, -1)):
            a, b = twist_cols[0, k1 : k1 + 1, :], twist_cols[1, k1 : k1 + 1, :]
            pieces.append(jnp.concatenate([re * a + im * b, im * a - re * b], axis=1))
    result = dot_left(tables, COLS_FWD, jnp.concatenate(pieces, axis=0), 1).astype(BF16)
    for l in range(2):
        send1[:, l * 32 : l * 32 + 32, :] = result[:, l * 128 : l * 128 + 128].reshape(8, 32, 128)
    recv1[yc] = send1[yc]

    pl.semaphore_wait(barrier, len(far) + len(near) + len(across))

    def exchange_near(send, recv, slot_of, send_sem, recv_sem):
        copies = []
        for n, (ny, nc) in enumerate(near):
            copy = pltpu.make_async_remote_copy(
                src_ref=send.at[slot_of(ny, nc)],
                dst_ref=recv.at[yc],
                send_sem=send_sem.at[n],
                recv_sem=recv_sem.at[n],
                device_id=(slab_of(ny, z, nc), led),
                device_id_type=MESH,
            )
            copy.start()
            copies.append(copy)
        return copies

    def exchange_far(send, recv, send_sem, recv_sem):
        copies = []
        for n, nz in enumerate(far):
            copy = pltpu.make_async_remote_copy(
                src_ref=send.at[nz],
                dst_ref=recv.at[z],
                send_sem=send_sem.at[n],
                recv_sem=recv_sem.at[n],
                device_id=(slab_of(y, nz, core), led),
                device_id_type=MESH,
            )
            copy.start()
            copies.append(copy)
        return copies

    copies1 = exchange_near(send1, recv1, lambda ny, nc: ny * NC + nc, s1, r1)

    for load in loads[3:]:
        load.wait()
    moduli = []
    for l in range(2):
        stacked = jnp.concatenate(
            [img[l, :, q * 64 : q * 64 + 64] for q in range(16)], axis=0
        )
        moduli.append(jnp.sqrt(stacked).T)
    moduli = jnp.concatenate(moduli, axis=0)
    tw_re, tw_im = twist_rows[0], twist_rows[1]

    for copy in copies1:
        copy.wait_recv()
    moved = dot(tables[FOLD], recv1[0:4].reshape(256, 128)) + dot(
        tables[FOLD + 1], recv1[4:8].reshape(256, 128)
    )
    send2[...] = moved.astype(BF16).reshape(16, 16, 128)
    recv2[z] = send2[z]
    copies2 = exchange_far(send2, recv2, s2, r2)
    for copy in copies2:
        copy.wait_recv()

    strips = recv2[...].reshape(256, 128)
    mixed = dot(tables[ROWS_FWD], strips) + dot(tables[ROWS_FWD + 1], strips)
    rows = []
    for l in range(2):
        re, im = mixed[l * 128 : l * 128 + 64], mixed[l * 128 + 64 : l * 128 + 128]
        rows.append(
            jnp.concatenate([re * tw_re + im * tw_im, im * tw_re - re * tw_im], axis=1)
        )
    field = dot_right(jnp.concatenate(rows, axis=0), tables, SHORT_FWD)
    field_re, field_im = field[:, :128], field[:, 128:]
    factor = moduli / jnp.sqrt(field_re * field_re + field_im * field_im + 0.25) - 1.0
    change = jnp.concatenate([field_re * factor, field_im * factor], axis=1)
    back = dot_right(change, tables, SHORT_INV)
    rows = []
    for l in range(2):
        re, im = back[l * 64 : l * 64 + 64, :128], back[l * 64 : l * 64 + 64, 128:]
        rows.append(re * tw_re - im * tw_im)
        rows.append(im * tw_re + re * tw_im)
    result = dot_left(tables, ROWS_INV, jnp.concatenate(rows, axis=0))
    send3[...] = result.astype(BF16).reshape(16, 16, 128)
    recv3[z] = send3[z]
    copies3 = exchange_far(send3, recv3, s3, r3)
    for copy in copies3:
        copy.wait_recv()

    moved = dot(tables[SWAP], recv3[...].reshape(256, 128))
    send4[...] = moved.astype(BF16).reshape(4, 64, 128)
    own_slot = lax.rem(y, 2) * NC + core
    recv4[yc] = send4[own_slot]
    copies4 = exchange_near(send4, recv4, lambda ny, nc: lax.rem(ny, 2) * NC + nc, s4, r4)
    for copy in copies4:
        copy.wait_recv()

    home = jnp.concatenate(
        [recv4[:, l * 32 : l * 32 + 32, :].reshape(256, 128) for l in range(2)], axis=1
    )
    spread = dot(tables[COLS_INV], home) + dot(tables[COLS_INV + 1], home)
    updates = []
    for l in range(2):
        re = spread[:128, l * 128 : l * 128 + 128].T
        im = spread[128:, l * 128 : l * 128 + 128].T
        values = []
        for k1 in range(8):
            a, b = twist_cols[0, k1 : k1 + 1, :], twist_cols[1, k1 : k1 + 1, :]
            kr, ki = re[k1 * 16 : k1 * 16 + 16], im[k1 * 16 : k1 * 16 + 16]
            values.append((kr * a - ki * b, ki * a + kr * b))
        updates.append(fft(values, 1))
    for block in range(16):
        masks = [inside(l, block) for l in range(2)]
        for part in range(2):
            total = jnp.where(masks[0], updates[0][block % 8][part], 0.0) + jnp.where(
                masks[1], updates[1][block % 8][part], 0.0
            )
            lanes = slice(block % 4 * 128, block % 4 * 128 + 128)
            grad[block // 4, part, :, lanes] = total
            send5[block // 4, part, :, lanes] = total.astype(BF16)
    copies5 = []
    for n, nx in enumerate(across):
        copy = pltpu.make_async_remote_copy(
            src_ref=send5.at[nx],
            dst_ref=recv5.at[n],
            send_sem=s5.at[n],
            recv_sem=r5.at[n],
            device_id=(slab, nx),
            device_id_type=MESH,
        )
        copy.start()
        copies5.append(copy)
    share = out.shape[2]
    total = spec[:, :, pl.ds(pl.multiple_of(led * share, share), share)] + grad[led]
    for n, copy in enumerate(copies5):
        copy.wait_recv()
    for n in range(3):
        total = total + recv5[n].astype(F32)
    out[...] = total
    for copy in copies1 + copies2 + copies3 + copies4 + copies5:
        copy.wait_send()


def body(tables, twist_cols, twist_rows, spectrum, led_rows, led_cols, images):
    smem = pl.BlockSpec(memory_space=pltpu.SMEM)
    here = pl.BlockSpec(memory_space=pl.ANY)
    columns = spectrum.shape[2]
    share = columns // NX
    return pl.pallas_call(
        step_kernel,
        out_shape=jax.ShapeDtypeStruct((2, 16, share), F32),
        in_specs=[smem, smem] + [here] * 5,
        out_specs=pl.BlockSpec(memory_space=pltpu.VMEM),
        scratch_shapes=[
            pltpu.VMEM((2, 16, columns), F32),
            pltpu.VMEM((2, 8, WIN), F32),
            pltpu.VMEM(tables.shape, BF16),
            pltpu.VMEM(twist_cols.shape, F32),
            pltpu.VMEM(twist_rows.shape, F32),
            pltpu.VMEM((NX, 2, 16, share), F32),
            pltpu.VMEM((8, 64, 128), BF16),
            pltpu.VMEM((8, 64, 128), BF16),
            pltpu.VMEM((16, 16, 128), BF16),
            pltpu.VMEM((16, 16, 128), BF16),
            pltpu.VMEM((16, 16, 128), BF16),
            pltpu.VMEM((16, 16, 128), BF16),
            pltpu.VMEM((4, 64, 128), BF16),
            pltpu.VMEM((8, 64, 128), BF16),
            pltpu.VMEM((NX, 2, 16, share), BF16),
            pltpu.VMEM((3, 2, 16, share), BF16),
            pltpu.SemaphoreType.DMA((6,)),
        ]
        + [pltpu.SemaphoreType.DMA((n,)) for n in (7, 7, 15, 15, 15, 15, 7, 7, 3, 3)],
        compiler_params=pltpu.CompilerParams(collective_id=0, has_side_effects=True),
        name="ptychography_step",
    )(led_rows, led_cols, spectrum, images, tables, twist_cols, twist_rows)


def solution(mesh):
    tables = make_tables()
    placed = (P(None, "slab", None), P("led"), P("led"), P("led", "slab", None))
    mapped = jax.shard_map(
        body,
        mesh=mesh,
        in_specs=(P(), P(), P()) + placed,
        out_specs=P(None, "slab", "led"),
        check_vma=False,
    )

    def step(spectrum, led_rows, led_cols, images):
        constants = [jnp.asarray(table) for table in tables]
        return mapped(*constants, spectrum, led_rows, led_cols, images)

    return step
```

profile of v0, /device:TPU:1, one launch (start us, length us, event | category | flops | bytes accessed | tf_op | source)
XLA Modules:
  0.0 48.0 jit_solution(8927384401410893736)
XLA Ops:
  0.0 46.6 %ptychography_step.1 = f32[2,16,512]{2,1,0:T(8,128)} custom-call(s32[2]{0:T(128)} %led_rows.1, s32[2]{0:T(128)} %led_cols.1, f32[2,16,2048]{2,1,0:T(8,128)} %spectrum.1, f32[2,8,1024]{2,1,0:T(8,128)} %images.1, bf16[15,256,256]{2,1,0:T(8,128)(2,1)} %constant.6.clone.tables_in, f32[2,8,128]{2,1,0:T(8,128)} %constant.7.clone.twist_cols_in, ...), custom_call_target="tpu_custom_call" | custom-call | tf_op jit(solution)/shard_map/ptychography_step/pallas_call | solution.py:345
  46.6 1.5 %copy.9 = f32[2,16,512]{2,1,0:T(8,128)} copy(f32[2,16,512]{2,1,0:T(8,128)} %ptychography_step.1) | data formatting | bytes 131072
where the time goes:
time: 48.2 us; the launch traced here: 48 us
  Pallas kernels  46.6 us (97%)
  local copies, waits for them, and re-layouts  1.47 us (3%)
    pallas_call x1, Pallas kernels, body(): pl.pallas_call(step_kernel, out_shape=jax.ShapeDtypeStruct((2, 16, share)...  46.6 us
    unnamed x1, local copies, waits for them, and re-layouts  1.47 us

commit v1 on v0

--- a/solution.py
+++ b/solution.py
@@ -120,8 +120,8 @@
 
 
 def step_kernel(
-    led_rows, led_cols, spectrum, images, tables_in, twist_cols_in, twist_rows_in, out,
-    spec, img, tables, twist_cols, twist_rows, grad,
+    rows_in, cols_in, spectrum, images, tables_in, twist_cols_in, twist_rows_in, out,
+    led_rows, led_cols, spec, img, tables, twist_cols, twist_rows, grad,
     send1, recv1, send2, recv2, send3, recv3, send4, recv4, send5, recv5,
     in_sem, s1, r1, s2, r2, s3, r3, s4, r4, s5, r5,
 ):
@@ -140,23 +140,13 @@
     far = [lax.rem(z + dz, NZ) for dz in far]
     across = [lax.rem(led + dx, NX) for dx in (2, 1, 3)]
 
-    barrier = pltpu.get_barrier_semaphore()
-    for nz in far:
-        pl.semaphore_signal(
-            barrier, inc=1, device_id=(slab_of(y, nz, core), led), device_id_type=MESH
-        )
-    for ny, nc in near:
-        pl.semaphore_signal(
-            barrier, inc=1, device_id=(slab_of(ny, z, nc), led), device_id_type=MESH
-        )
-    for nx in across:
-        pl.semaphore_signal(barrier, inc=1, device_id=(slab, nx), device_id_type=MESH)
-
     loads = [
         pltpu.make_async_copy(a, b, in_sem.at[n])
         for n, (a, b) in enumerate(
             [
                 (spectrum, spec),
+                (rows_in, led_rows),
+                (cols_in, led_cols),
                 (twist_cols_in, twist_cols),
                 (tables_in.at[0:2], tables.at[0:2]),
                 (images, img),
@@ -168,19 +158,31 @@
     for load in loads:
         load.start()
 
+    barrier = pltpu.get_barrier_semaphore()
+    for nz in far:
+        pl.semaphore_signal(
+            barrier, inc=1, device_id=(slab_of(y, nz, core), led), device_id_type=MESH
+        )
+    for ny, nc in near:
+        pl.semaphore_signal(
+            barrier, inc=1, device_id=(slab_of(ny, z, nc), led), device_id_type=MESH
+        )
+    for nx in across:
+        pl.semaphore_signal(barrier, inc=1, device_id=(slab, nx), device_id_type=MESH)
+
     row_at = slab * 16 + lax.broadcasted_iota(jnp.int32, (16, 128), 0)
     lane = lax.broadcasted_iota(jnp.int32, (16, 128), 1)
 
     def term(offset):
         return (2 * offset + 1 - WIN) * (2 * offset + 1 - WIN)
 
-    row_terms = [term(row_at - led_rows[l]) for l in range(2)]
-
     def inside(l, block):
         return row_terms[l] + term(lane + (block * 128 - led_cols[l])) < WIN * WIN
 
-    for load in loads[:3]:
-        load.wait()
+    with jax.named_scope("wait_load"):
+        for load in loads[:5]:
+            load.wait()
+    row_terms = [term(row_at - led_rows[l]) for l in range(2)]
     pieces = []
     for l in range(2):
         values = []
@@ -202,7 +204,8 @@
         send1[:, l * 32 : l * 32 + 32, :] = result[:, l * 128 : l * 128 + 128].reshape(8, 32, 128)
     recv1[yc] = send1[yc]
 
-    pl.semaphore_wait(barrier, len(far) + len(near) + len(across))
+    with jax.named_scope("wait_barrier"):
+        pl.semaphore_wait(barrier, len(far) + len(near) + len(across))
 
     def exchange_near(send, recv, slot_of, send_sem, recv_sem):
         copies = []
@@ -236,7 +239,7 @@
 
     copies1 = exchange_near(send1, recv1, lambda ny, nc: ny * NC + nc, s1, r1)
 
-    for load in loads[3:]:
+    for load in loads[5:]:
         load.wait()
     moduli = []
     for l in range(2):
@@ -247,16 +250,18 @@
     moduli = jnp.concatenate(moduli, axis=0)
     tw_re, tw_im = twist_rows[0], twist_rows[1]
 
-    for copy in copies1:
-        copy.wait_recv()
+    with jax.named_scope("wait_1"):
+        for copy in copies1:
+            copy.wait_recv()
     moved = dot(tables[FOLD], recv1[0:4].reshape(256, 128)) + dot(
         tables[FOLD + 1], recv1[4:8].reshape(256, 128)
     )
     send2[...] = moved.astype(BF16).reshape(16, 16, 128)
     recv2[z] = send2[z]
     copies2 = exchange_far(send2, recv2, s2, r2)
-    for copy in copies2:
-        copy.wait_recv()
+    with jax.named_scope("wait_2"):
+        for copy in copies2:
+            copy.wait_recv()
 
     strips = recv2[...].reshape(256, 128)
     mixed = dot(tables[ROWS_FWD], strips) + dot(tables[ROWS_FWD + 1], strips)
@@ -280,16 +285,18 @@
     send3[...] = result.astype(BF16).reshape(16, 16, 128)
     recv3[z] = send3[z]
     copies3 = exchange_far(send3, recv3, s3, r3)
-    for copy in copies3:
-        copy.wait_recv()
+    with jax.named_scope("wait_3"):
+        for copy in copies3:
+            copy.wait_recv()
 
     moved = dot(tables[SWAP], recv3[...].reshape(256, 128))
     send4[...] = moved.astype(BF16).reshape(4, 64, 128)
     own_slot = lax.rem(y, 2) * NC + core
     recv4[yc] = send4[own_slot]
     copies4 = exchange_near(send4, recv4, lambda ny, nc: lax.rem(ny, 2) * NC + nc, s4, r4)
-    for copy in copies4:
-        copy.wait_recv()
+    with jax.named_scope("wait_4"):
+        for copy in copies4:
+            copy.wait_recv()
 
     home = jnp.concatenate(
         [recv4[:, l * 32 : l * 32 + 32, :].reshape(256, 128) for l in range(2)], axis=1
@@ -328,8 +335,9 @@
         copies5.append(copy)
     share = out.shape[2]
     total = spec[:, :, pl.ds(pl.multiple_of(led * share, share), share)] + grad[led]
-    for n, copy in enumerate(copies5):
-        copy.wait_recv()
+    with jax.named_scope("wait_5"):
+        for copy in copies5:
+            copy.wait_recv()
     for n in range(3):
         total = total + recv5[n].astype(F32)
     out[...] = total
@@ -338,16 +346,17 @@
 
 
 def body(tables, twist_cols, twist_rows, spectrum, led_rows, led_cols, images):
-    smem = pl.BlockSpec(memory_space=pltpu.SMEM)
     here = pl.BlockSpec(memory_space=pl.ANY)
     columns = spectrum.shape[2]
     share = columns // NX
     return pl.pallas_call(
         step_kernel,
-        out_shape=jax.ShapeDtypeStruct((2, 16, share), F32),
-        in_specs=[smem, smem] + [here] * 5,
+        out_shape=pltpu.VMEM((2, 16, share), F32),
+        in_specs=[here] * 7,
         out_specs=pl.BlockSpec(memory_space=pltpu.VMEM),
         scratch_shapes=[
+            pltpu.SMEM((2,), jnp.int32),
+            pltpu.SMEM((2,), jnp.int32),
             pltpu.VMEM((2, 16, columns), F32),
             pltpu.VMEM((2, 8, WIN), F32),
             pltpu.VMEM(tables.shape, BF16),
@@ -364,7 +373,7 @@
             pltpu.VMEM((8, 64, 128), BF16),
             pltpu.VMEM((NX, 2, 16, share), BF16),
             pltpu.VMEM((3, 2, 16, share), BF16),
-            pltpu.SemaphoreType.DMA((6,)),
+            pltpu.SemaphoreType.DMA((8,)),
         ]
         + [pltpu.SemaphoreType.DMA((n,)) for n in (7, 7, 15, 15, 15, 15, 7, 7, 3, 3)],
         compiler_params=pltpu.CompilerParams(collective_id=0, has_side_effects=True),

time: 48.2 us -> 46.1 us (0.956)
  Pallas kernels: 46.6 us -> 45.3 us
  local copies, waits for them, and re-layouts: 1.47 us -> 0.63 us
    pallas_call x1, Pallas kernels: 46.6 us -> 45.3 us  [body(): pl.pallas_call(step_kernel, out_shape=pltpu.VMEM((2, 16, share), F32), in...]
    unnamed x1, local copies, waits for them, and re-layouts: 1.47 us -> 0.63 us
where the time goes in v1:
time: 46.1 us; the launch traced here: 46 us
  Pallas kernels  45.3 us (98%)
  local copies, waits for them, and re-layouts  0.63 us (1%)
    pallas_call x1, Pallas kernels, body(): pl.pallas_call(step_kernel, out_shape=pltpu.VMEM((2, 16, share), F32), in...  45.3 us

profile of v1, /device:TPU:1, one launch (start us, length us, event | category | flops | bytes accessed | tf_op | source)
XLA Modules:
  0.0 46.0 jit_solution(3410673752660808561)
XLA Ops:
  0.0 45.3 %ptychography_step.1 = f32[2,16,512]{2,1,0:T(8,128)S(1)} custom-call(s32[2]{0:T(128)} %rows_in.1, s32[2]{0:T(128)} %cols_in.1, f32[2,16,2048]{2,1,0:T(8,128)} %spectrum.1, f32[2,8,1024]{2,1,0:T(8,128)} %images.1, bf16[15,256,256]{2,1,0:T(8,128)(2,1)} %constant.6.clone.tables_in, f32[2,8,128]{2,1,0:T(8,128)} %constant.7.clone.twist_cols_in, ...), custom_call_target="tpu_custom_call" | custom-call | tf_op jit(solution)/shard_map/ptychography_step/pallas_call | solution.py:352
  45.3 0.6 %copy.9 = f32[2,16,512]{2,1,0:T(8,128)} copy(f32[2,16,512]{2,1,0:T(8,128)S(1)} %ptychography_step.1) | data formatting | bytes 131072

commit v2 on v1

v2 whole, which is shorter than its diff:
```python
import functools

import jax
import jax.numpy as jnp
import numpy as np
from jax import lax
from jax.experimental import pallas as pl
from jax.experimental.pallas import tpu as pltpu
from jax.sharding import PartitionSpec as P

NY, NZ, NC, NX = 4, 16, 2, 4
WIN = 1024
MESH = pl.DeviceIdType.MESH
F32, BF16 = jnp.float32, jnp.bfloat16


def grid_of(*sizes):
    return np.meshgrid(*[np.arange(n) for n in sizes], indexing="ij")


def rotation(angle_index, period, out_part, in_part, sign):
    angle = 2.0 * np.pi * (angle_index % period) / period
    same = np.cos(angle)
    cross = sign * np.sin(angle)
    return np.where(out_part == in_part, same, np.where(out_part == 1, cross, -cross))


def split(table):
    high = np.asarray(table, np.float32).astype(BF16)
    low = (table - high.astype(np.float64)).astype(np.float32).astype(BF16)
    return high, low


def make_tables():
    scale = 1.0 / 32.0
    y, c, po, z, pi, n2 = grid_of(NY, NC, 2, NZ, 2, 128)
    k2 = (y * NZ + z) * NC + c
    cols_fwd = scale * rotation(k2 * n2, 128, po, pi, -1).reshape(256, 256)
    z, yb, c, p, y2, c2, p2, z2 = grid_of(NZ, 2, NC, 2, NY, NC, 2, NZ)
    hit = (z == z2) & (p == p2) & (c == c2) & (y2 % 2 == yb)
    fold = hit.astype(np.float64).reshape(128, 256)
    po, p, z, yb, c, pi = grid_of(2, 64, NZ, 2, NC, 2)
    strip = 32 * yb + 2 * z + c
    rows_fwd = scale * rotation(strip * p, 64, po, pi, -1).reshape(128, 128)
    z, yb, c, po, pi, p = grid_of(NZ, 2, NC, 2, 2, 64)
    strip = 32 * yb + 2 * z + c
    rows_inv = scale * rotation(strip * p, 64, po, pi, 1).reshape(128, 128)
    pi, k1, i, po, q, k1o = grid_of(2, 8, 16, 2, 16, 8)
    short_fwd = (rotation(i * q, 16, po, pi, -1) * (k1 == k1o)).reshape(256, 256)
    pi, q, k1, po, k1o, i = grid_of(2, 16, 8, 2, 8, 16)
    short_inv = (rotation(i * q, 16, po, pi, 1) * (k1 == k1o)).reshape(256, 256)
    yb, c, p, z, z2, yb2, c2, p2 = grid_of(2, NC, 2, NZ, NZ, 2, NC, 2)
    hit = (z == z2) & (p == p2) & (c == c2) & (yb == yb2)
    swap = hit.astype(np.float64).reshape(128, 128)
    po, n2, y, c, pi, z = grid_of(2, 128, NY, NC, 2, NZ)
    k2 = (y * NZ + z) * NC + c
    cols_inv = scale * rotation(k2 * n2, 128, po, pi, 1).reshape(256, 256)
    wide, small = [], []
    for table in (cols_fwd, short_fwd, short_inv, cols_inv):
        wide.extend(split(table))
    for table in (rows_fwd, rows_inv):
        small.extend(split(table))
    for table in (fold[:, :128], fold[:, 128:], swap):
        small.append(np.asarray(table, np.float32).astype(BF16))
    k1, n2 = grid_of(8, 128)
    angle = 2.0 * np.pi * ((k1 * n2) % WIN) / WIN
    twist_cols = np.stack([np.cos(angle), np.sin(angle)]).astype(np.float32)
    p, k1, i = grid_of(64, 8, 16)
    angle = (2.0 * np.pi * ((p * i) % WIN) / WIN).reshape(64, 128)
    twist_rows = np.stack([np.cos(angle), np.sin(angle)]).astype(np.float32)
    return np.stack(wide), np.stack(small), twist_cols, twist_rows


COLS_FWD, SHORT_FWD, SHORT_INV, COLS_INV = range(0, 8, 2)
ROWS_FWD, ROWS_INV, FOLD, SWAP = 0, 2, 4, 6
LINKS = (1, 3, 4)


def fft(values, sign):
    size = len(values)
    if size == 1:
        return values
    even, odd = fft(values[0::2], sign), fft(values[1::2], sign)
    low, high = [], []
    for k in range(size // 2):
        (er, ei), (re, im) = even[k], odd[k]
        if k == 0:
            tr, ti = re, im
        elif 4 * k == size:
            tr, ti = (-im, re) if sign > 0 else (im, -re)
        else:
            a = float(np.cos(2 * np.pi * k / size))
            b = float(np.sin(2 * np.pi * k / size)) * sign
            tr, ti = a * re - b * im, a * im + b * re
        low.append((er + tr, ei + ti))
        high.append((er - tr, ei - ti))
    return low + high


def halves(value):
    high = value.astype(BF16)
    return high, (value - high.astype(F32)).astype(BF16)


def dot(left, right, right_dim=0):
    return lax.dot_general(
        left, right, (((1,), (right_dim,)), ((), ())), preferred_element_type=F32
    )


def dot_left(tables, at, value, right_dim=0):
    high, low = halves(value)
    return (
        dot(tables[at], high, right_dim)
        + dot(tables[at + 1], high, right_dim)
        + dot(tables[at], low, right_dim)
    )


def dot_right(value, tables, at):
    high, low = halves(value)
    return dot(high, tables[at]) + dot(low, tables[at]) + dot(high, tables[at + 1])


def step_kernel(
    rows_in, cols_in, spectrum, images, wide_in, small_in, twist_cols_in, twist_rows_in, out,
    led_rows, led_cols, spec, img, wide, small, twist_cols, twist_rows, grad,
    send1, recv1, send2, recv2, send3, recv3, send4, recv4, send5, recv5,
    in_sem, known, s1, r1, s2, r2, s3, r3, s4, r4, s5, r5,
):
    slab, led = lax.axis_index("slab"), lax.axis_index("led")
    core = lax.rem(slab, NC)
    z = lax.rem(lax.div(slab, NC), NZ)
    y = lax.div(slab, NC * NZ)
    yc = y * NC + core

    def slab_of(ny, nz, nc):
        return (ny * NZ + nz) * NC + nc

    near = [(2, 1), (2, 0), (1, 1), (3, 1), (1, 0), (3, 0), (0, 1)]
    near = [(lax.rem(y + dy, NY), lax.rem(core + dc, NC)) for dy, dc in near]
    far = [8, 7, 9, 6, 10, 5, 11, 4, 12, 3, 13, 2, 14, 1, 15]
    far = [lax.rem(z + dz, NZ) for dz in far]
    links = [lax.rem(z + dz, NZ) for d in LINKS for dz in (d, NZ - d)]
    across = [lax.rem(led + dx, NX) for dx in (2, 1, 3)]

    loads = [
        pltpu.make_async_copy(a, b, in_sem.at[n])
        for n, (a, b) in enumerate(
            [
                (spectrum, spec),
                (rows_in, led_rows),
                (cols_in, led_cols),
                (twist_cols_in, twist_cols),
                (wide_in.at[0:2], wide.at[0:2]),
                (images, img),
                (twist_rows_in, twist_rows),
                (small_in, small),
                (wide_in.at[2:8], wide.at[2:8]),
            ]
        )
    ]
    for load in loads:
        load.start()
    barrier = pltpu.get_barrier_semaphore()

    def greet_links(semaphore):
        for nz in links:
            pl.semaphore_signal(
                semaphore, inc=1, device_id=(slab_of(y, nz, core), led), device_id_type=MESH
            )

    greet_links(barrier)
    for ny, nc in near:
        pl.semaphore_signal(
            barrier, inc=1, device_id=(slab_of(ny, z, nc), led), device_id_type=MESH
        )
    for nx in across:
        pl.semaphore_signal(barrier, inc=1, device_id=(slab, nx), device_id_type=MESH)

    row_at = slab * 16 + lax.broadcasted_iota(jnp.int32, (16, 128), 0)
    lane = lax.broadcasted_iota(jnp.int32, (16, 128), 1)

    def term(offset):
        return (2 * offset + 1 - WIN) * (2 * offset + 1 - WIN)

    def inside(l, block):
        return row_terms[l] + term(lane + (block * 128 - led_cols[l])) < WIN * WIN

    def exchange(n_peers, source_of, target, peer_of, send_sem, recv_sem):
        copies = []
        for n in range(n_peers):
            copy = pltpu.make_async_remote_copy(
                src_ref=source_of(n),
                dst_ref=target(n),
                send_sem=send_sem.at[n],
                recv_sem=recv_sem.at[n],
                device_id=peer_of(n),
                device_id_type=MESH,
            )
            copy.start()
            copies.append(copy)
        return copies

    def near_peer(n):
        ny, nc = near[n]
        return slab_of(ny, z, nc), led

    def far_peer(n):
        return slab_of(y, far[n], core), led

    def arrived(name, copies):
        with jax.named_scope(name):
            for copy in copies:
                copy.wait_recv()

    with jax.named_scope("wait_load"):
        for load in loads[:5]:
            load.wait()
    row_terms = [term(row_at - led_rows[l]) for l in range(2)]
    for l in range(2):
        pieces = []
        values = []
        masks = [inside(l, block) for block in range(16)]
        for n1 in range(8):
            parts = []
            for part in range(2):
                first = spec[part, :, n1 * 128 : n1 * 128 + 128]
                second = spec[part, :, 1024 + n1 * 128 : 1152 + n1 * 128]
                parts.append(
                    jnp.where(masks[n1], first, 0.0) + jnp.where(masks[n1 + 8], second, 0.0)
                )
            values.append(tuple(parts))
        for k1, (re, im) in enumerate(fft(values, -1)):
            a, b = twist_cols[0, k1 : k1 + 1, :], twist_cols[1, k1 : k1 + 1, :]
            pieces.append(jnp.concatenate([re * a + im * b, im * a - re * b], axis=1))
        result = dot_left(wide, COLS_FWD, jnp.concatenate(pieces, axis=0), 1)
        send1[l] = result.astype(BF16).reshape(8, 32, 128)
        recv1[l, yc] = send1[l, yc]

    with jax.named_scope("wait_barrier"):
        pl.semaphore_wait(barrier, len(links) + len(near) + len(across))
    greet_links(known)
    copies1 = [
        exchange(
            len(near),
            lambda n: send1.at[l, near[n][0] * NC + near[n][1]],
            lambda n: recv1.at[l, yc],
            near_peer,
            s1.at[l],
            r1.at[l],
        )
        for l in range(2)
    ]

    for load in loads[5:]:
        load.wait()
    moduli = []
    for l in range(2):
        stacked = jnp.concatenate(
            [img[l, :, q * 64 : q * 64 + 64] for q in range(16)], axis=0
        )
        moduli.append(jnp.sqrt(stacked).T)
    tw_re, tw_im = twist_rows[0], twist_rows[1]

    copies2 = []
    for l in range(2):
        arrived("wait_1%d" % l, copies1[l])
        moved = dot(small[FOLD], recv1[l, 0:4].reshape(128, 128)) + dot(
            small[FOLD + 1], recv1[l, 4:8].reshape(128, 128)
        )
        send2[l] = moved.astype(BF16).reshape(16, 8, 128)
        recv2[l, z] = send2[l, z]
        if l == 0:
            with jax.named_scope("wait_known"):
                pl.semaphore_wait(known, len(links))
        copies2.append(
            exchange(
                len(far),
                lambda n: send2.at[l, far[n]],
                lambda n: recv2.at[l, z],
                far_peer,
                s2.at[l],
                r2.at[l],
            )
        )

    copies3 = []
    for l in range(2):
        arrived("wait_2%d" % l, copies2[l])
        strips = recv2[l].reshape(128, 128)
        mixed = dot(small[ROWS_FWD], strips) + dot(small[ROWS_FWD + 1], strips)
        re, im = mixed[:64], mixed[64:]
        rows = jnp.concatenate([re * tw_re + im * tw_im, im * tw_re - re * tw_im], axis=1)
        field = dot_right(rows, wide, SHORT_FWD)
        field_re, field_im = field[:, :128], field[:, 128:]
        factor = moduli[l] / jnp.sqrt(field_re * field_re + field_im * field_im + 0.25) - 1.0
        change = jnp.concatenate([field_re * factor, field_im * factor], axis=1)
        back = dot_right(change, wide, SHORT_INV)
        re, im = back[:, :128], back[:, 128:]
        rows = jnp.concatenate([re * tw_re - im * tw_im, im * tw_re + re * tw_im], axis=0)
        result = dot_left(small, ROWS_INV, rows)
        send3[l] = result.astype(BF16).reshape(16, 8, 128)
        recv3[l, z] = send3[l, z]
        copies3.append(
            exchange(
                len(far),
                lambda n: send3.at[l, far[n]],
                lambda n: recv3.at[l, z],
                far_peer,
                s3.at[l],
                r3.at[l],
            )
        )

    copies4 = []
    for l in range(2):
        arrived("wait_3%d" % l, copies3[l])
        moved = dot(small[SWAP], recv3[l].reshape(128, 128))
        send4[l] = moved.astype(BF16).reshape(4, 32, 128)
        recv4[l, yc] = send4[l, lax.rem(y, 2) * NC + core]
        copies4.append(
            exchange(
                len(near),
                lambda n: send4.at[l, lax.rem(near[n][0], 2) * NC + near[n][1]],
                lambda n: recv4.at[l, yc],
                near_peer,
                s4.at[l],
                r4.at[l],
            )
        )

    updates = []
    for l in range(2):
        arrived("wait_4%d" % l, copies4[l])
        home = recv4[l].reshape(256, 128)
        spread = dot(wide[COLS_INV], home) + dot(wide[COLS_INV + 1], home)
        re, im = spread[:128].T, spread[128:].T
        values = []
        for k1 in range(8):
            a, b = twist_cols[0, k1 : k1 + 1, :], twist_cols[1, k1 : k1 + 1, :]
            kr, ki = re[k1 * 16 : k1 * 16 + 16], im[k1 * 16 : k1 * 16 + 16]
            values.append((kr * a - ki * b, ki * a + kr * b))
        updates.append(fft(values, 1))
    for block in range(16):
        masks = [inside(l, block) for l in range(2)]
        for part in range(2):
            total = jnp.where(masks[0], updates[0][block % 8][part], 0.0) + jnp.where(
                masks[1], updates[1][block % 8][part], 0.0
            )
            lanes = slice(block % 4 * 128, block % 4 * 128 + 128)
            grad[block // 4, part, :, lanes] = total
            send5[block // 4, part, :, lanes] = total.astype(BF16)
    copies5 = exchange(
        len(across),
        lambda n: send5.at[across[n]],
        lambda n: recv5.at[n],
        lambda n: (slab, across[n]),
        s5,
        r5,
    )
    share = out.shape[2]
    total = spec[:, :, pl.ds(pl.multiple_of(led * share, share), share)] + grad[led]
    arrived("wait_5", copies5)
    for n in range(3):
        total = total + recv5[n].astype(F32)
    out[...] = total
    for copies in copies1 + copies2 + copies3 + copies4 + [copies5]:
        for copy in copies:
            copy.wait_send()


def body(wide, small, twist_cols, twist_rows, spectrum, led_rows, led_cols, images):
    columns = spectrum.shape[2]
    share = columns // NX
    pairs = [(2, 7), (2, 15), (2, 15), (2, 7), (3,)]
    return pl.pallas_call(
        step_kernel,
        out_shape=pltpu.VMEM((2, 16, share), F32),
        in_specs=[pl.BlockSpec(memory_space=pl.ANY)] * 8,
        out_specs=pl.BlockSpec(memory_space=pltpu.VMEM),
        scratch_shapes=[
            pltpu.SMEM((2,), jnp.int32),
            pltpu.SMEM((2,), jnp.int32),
            pltpu.VMEM((2, 16, columns), F32),
            pltpu.VMEM((2, 8, WIN), F32),
            pltpu.VMEM(wide.shape, BF16),
            pltpu.VMEM(small.shape, BF16),
            pltpu.VMEM(twist_cols.shape, F32),
            pltpu.VMEM(twist_rows.shape, F32),
            pltpu.VMEM((NX, 2, 16, share), F32),
            pltpu.VMEM((2, 8, 32, 128), BF16),
            pltpu.VMEM((2, 8, 32, 128), BF16),
            pltpu.VMEM((2, 16, 8, 128), BF16),
            pltpu.VMEM((2, 16, 8, 128), BF16),
            pltpu.VMEM((2, 16, 8, 128), BF16),
            pltpu.VMEM((2, 16, 8, 128), BF16),
            pltpu.VMEM((2, 4, 32, 128), BF16),
            pltpu.VMEM((2, 8, 32, 128), BF16),
            pltpu.VMEM((NX, 2, 16, share), BF16),
            pltpu.VMEM((3, 2, 16, share), BF16),
            pltpu.SemaphoreType.DMA((9,)),
            pltpu.SemaphoreType.REGULAR,
        ]
        + [pltpu.SemaphoreType.DMA(shape) for shape in pairs for _ in range(2)],
        compiler_params=pltpu.CompilerParams(collective_id=0, has_side_effects=True),
        name="ptychography_step",
    )(led_rows, led_cols, spectrum, images, wide, small, twist_cols, twist_rows)


def solution(mesh):
    tables = make_tables()
    placed = (P(None, "slab", None), P("led"), P("led"), P("led", "slab", None))
    mapped = jax.shard_map(
        body,
        mesh=mesh,
        in_specs=(P(),) * 4 + placed,
        out_specs=P(None, "slab", "led"),
        check_vma=False,
    )

    def step(spectrum, led_rows, led_cols, images):
        constants = [jnp.asarray(table) for table in tables]
        return mapped(*constants, spectrum, led_rows, led_cols, images)

    return step
```

time: 46.1 us -> 43.9 us (0.952)
  Pallas kernels: 45.3 us -> 43.1 us
    pallas_call x1, Pallas kernels: 45.3 us -> 43.1 us  [body(): pl.pallas_call(step_kernel, out_shape=pltpu.VMEM((2, 16, share), F32), in...]
where the time goes in v2:
time: 43.9 us; the launch traced here: 43.8 us
  Pallas kernels  43.1 us (98%)
  local copies, waits for them, and re-layouts  0.63 us (1%)
    pallas_call x1, Pallas kernels, body(): pl.pallas_call(step_kernel, out_shape=pltpu.VMEM((2, 16, share), F32), in...  43.1 us

profile of v2, /device:TPU:1, one launch (start us, length us, event | category | flops | bytes accessed | tf_op | source)
XLA Modules:
  0.0 43.8 jit_solution(11699983902898569344)
XLA Ops:
  0.0 43.1 %ptychography_step.1 = f32[2,16,512]{2,1,0:T(8,128)S(1)} custom-call(s32[2]{0:T(128)} %rows_in.1, s32[2]{0:T(128)} %cols_in.1, f32[2,16,2048]{2,1,0:T(8,128)} %spectrum.1, f32[2,8,1024]{2,1,0:T(8,128)} %images.1, bf16[8,256,256]{2,1,0:T(8,128)(2,1)} %constant.8.clone.wide_in, bf16[7,128,128]{2,1,0:T(8,128)(2,1)} %constant.9.clone.small_in, ...), custom_call_target="tpu_custom_call" | custom-call | tf_op jit(solution)/shard_map/ptychography_step/pallas_call | solution.py:377
  43.1 0.6 %copy.10 = f32[2,16,512]{2,1,0:T(8,128)} copy(f32[2,16,512]{2,1,0:T(8,128)S(1)} %ptychography_step.1) | data formatting | bytes 131072

commit v3 on v1

v3 whole, which is shorter than its diff:
```python
import functools

import jax
import jax.numpy as jnp
import numpy as np
from jax import lax
from jax.experimental import pallas as pl
from jax.experimental.pallas import tpu as pltpu
from jax.sharding import PartitionSpec as P

NY, NZ, NC, NX = 4, 16, 2, 4
WIN = 1024
MESH = pl.DeviceIdType.MESH
F32, BF16 = jnp.float32, jnp.bfloat16


def grid_of(*sizes):
    return np.meshgrid(*[np.arange(n) for n in sizes], indexing="ij")


def rotation(angle_index, period, out_part, in_part, sign):
    angle = 2.0 * np.pi * (angle_index % period) / period
    same = np.cos(angle)
    cross = sign * np.sin(angle)
    return np.where(out_part == in_part, same, np.where(out_part == 1, cross, -cross))


def split(table):
    high = np.asarray(table, np.float32).astype(BF16)
    low = (table - high.astype(np.float64)).astype(np.float32).astype(BF16)
    return high, low


def make_tables():
    scale = 1.0 / 32.0
    y, c, po, z, pi, n2 = grid_of(NY, NC, 2, NZ, 2, 128)
    k2 = (y * NZ + z) * NC + c
    cols_fwd = scale * rotation(k2 * n2, 128, po, pi, -1).reshape(256, 256)
    z, l, yb, c, p, y2, c2, l2, p2, z2 = grid_of(NZ, 2, 2, NC, 2, NY, NC, 2, 2, NZ)
    hit = (z == z2) & (l == l2) & (p == p2) & (c == c2) & (y2 % 2 == yb)
    fold = hit.astype(np.float64).reshape(256, 512)
    l, po, p, z, l2, yb, c, pi = grid_of(2, 2, 64, NZ, 2, 2, NC, 2)
    strip = 32 * yb + 2 * z + c
    rows_fwd = (scale * rotation(strip * p, 64, po, pi, -1) * (l == l2)).reshape(256, 256)
    strip, l, po, l2, pi, p = grid_of(64, 2, 2, 2, 2, 64)
    rows_inv = (scale * rotation(strip * p, 64, po, pi, 1) * (l == l2)).reshape(256, 256)
    pi, k1, i, po, q, k1o = grid_of(2, 8, 16, 2, 16, 8)
    short_fwd = (rotation(i * q, 16, po, pi, -1) * (k1 == k1o)).reshape(256, 256)
    pi, q, k1, po, k1o, i = grid_of(2, 16, 8, 2, 8, 16)
    short_inv = (rotation(i * q, 16, po, pi, 1) * (k1 == k1o)).reshape(256, 256)
    l, po, n2, k2, l2, pi = grid_of(2, 2, 128, 128, 2, 2)
    cols_inv = (scale * rotation(k2 * n2, 128, po, pi, 1) * (l == l2)).reshape(512, 512)
    wide = []
    for table in (cols_fwd, short_fwd, short_inv, rows_fwd, rows_inv):
        wide.extend(split(table))
    for table in (fold[:, :256], fold[:, 256:]):
        wide.append(np.asarray(table, np.float32).astype(BF16))
    k1, n2 = grid_of(8, 128)
    angle = 2.0 * np.pi * ((k1 * n2) % WIN) / WIN
    twist_cols = np.stack([np.cos(angle), np.sin(angle)]).astype(np.float32)
    p, k1, i = grid_of(64, 8, 16)
    angle = (2.0 * np.pi * ((p * i) % WIN) / WIN).reshape(64, 128)
    twist_rows = np.stack([np.cos(angle), np.sin(angle)]).astype(np.float32)
    return np.stack(wide), np.stack(split(cols_inv)), twist_cols, twist_rows


COLS_FWD, SHORT_FWD, SHORT_INV, ROWS_FWD, ROWS_INV, FOLD = range(0, 12, 2)
LINKS = (1, 3, 4)
HOPS = sorted(
    ((dy, dz, dc) for dy in range(NY) for dz in range(NZ) for dc in range(NC)),
    key=lambda d: -(min(d[0], NY - d[0]) + min(d[1], NZ - d[1]) + 0.1 * d[2]),
)[:-1]


def fft(values, sign):
    size = len(values)
    if size == 1:
        return values
    even, odd = fft(values[0::2], sign), fft(values[1::2], sign)
    low, high = [], []
    for k in range(size // 2):
        (er, ei), (re, im) = even[k], odd[k]
        if k == 0:
            tr, ti = re, im
        elif 4 * k == size:
            tr, ti = (-im, re) if sign > 0 else (im, -re)
        else:
            a = float(np.cos(2 * np.pi * k / size))
            b = float(np.sin(2 * np.pi * k / size)) * sign
            tr, ti = a * re - b * im, a * im + b * re
        low.append((er + tr, ei + ti))
        high.append((er - tr, ei - ti))
    return low + high


def halves(value):
    high = value.astype(BF16)
    return high, (value - high.astype(F32)).astype(BF16)


def dot(left, right, right_dim=0):
    return lax.dot_general(
        left, right, (((1,), (right_dim,)), ((), ())), preferred_element_type=F32
    )


def dot_left(tables, at, value, right_dim=0):
    high, low = halves(value)
    return (
        dot(tables[at], high, right_dim)
        + dot(tables[at + 1], high, right_dim)
        + dot(tables[at], low, right_dim)
    )


def dot_right(value, tables, at):
    high, low = halves(value)
    return dot(high, tables[at]) + dot(low, tables[at]) + dot(high, tables[at + 1])


def step_kernel(
    rows_in, cols_in, spectrum, images, wide_in, cols_inv_in, twist_cols_in, twist_rows_in, out,
    led_rows, led_cols, spec, img, wide, cols_inv, twist_cols, twist_rows, grad,
    send1, recv1, send2, recv2, send3, recv3, send5, recv5,
    in_sem, known, sent, got,
):
    slab, led = lax.axis_index("slab"), lax.axis_index("led")
    core = lax.rem(slab, NC)
    z = lax.rem(lax.div(slab, NC), NZ)
    y = lax.div(slab, NC * NZ)
    yc = y * NC + core

    def slab_of(ny, nz, nc):
        return (ny * NZ + nz) * NC + nc

    near = [(2, 1), (2, 0), (1, 1), (3, 1), (1, 0), (3, 0), (0, 1)]
    near = [(lax.rem(y + dy, NY), lax.rem(core + dc, NC)) for dy, dc in near]
    far = [8, 7, 9, 6, 10, 5, 11, 4, 12, 3, 13, 2, 14, 1, 15]
    far = [lax.rem(z + dz, NZ) for dz in far]
    across = [lax.rem(led + dx, NX) for dx in (2, 1, 3)]

    loads = [
        pltpu.make_async_copy(a, b, in_sem.at[n])
        for n, (a, b) in enumerate(
            [
                (spectrum, spec),
                (rows_in, led_rows),
                (cols_in, led_cols),
                (twist_cols_in, twist_cols),
                (wide_in.at[0:2], wide.at[0:2]),
                (images, img),
                (twist_rows_in, twist_rows),
                (wide_in.at[2:12], wide.at[2:12]),
                (cols_inv_in, cols_inv),
            ]
        )
    ]
    for load in loads[:5]:
        load.start()
    barrier = pltpu.get_barrier_semaphore()

    links = [lax.rem(z + dz, NZ) for d in LINKS for dz in (d, NZ - d)]

    def greet_links(semaphore):
        for nz in links:
            pl.semaphore_signal(
                semaphore, inc=1, device_id=(slab_of(y, nz, core), led), device_id_type=MESH
            )

    greet_links(barrier)
    for ny, nc in near:
        pl.semaphore_signal(
            barrier, inc=1, device_id=(slab_of(ny, z, nc), led), device_id_type=MESH
        )
    for nx in across:
        pl.semaphore_signal(barrier, inc=1, device_id=(slab, nx), device_id_type=MESH)
    for load in loads[5:]:
        load.start()

    row_at = slab * 16 + lax.broadcasted_iota(jnp.int32, (16, 128), 0)
    lane = lax.broadcasted_iota(jnp.int32, (16, 128), 1)

    def term(offset):
        return (2 * offset + 1 - WIN) * (2 * offset + 1 - WIN)

    def inside(l, block):
        return row_terms[l] + term(lane + (block * 128 - led_cols[l])) < WIN * WIN

    def exchange(n_peers, source_of, target_of, peer_of, at):
        for n in range(n_peers):
            pltpu.make_async_remote_copy(
                src_ref=source_of(n),
                dst_ref=target_of(n),
                send_sem=sent.at[at],
                recv_sem=got.at[at],
                device_id=peer_of(n),
                device_id_type=MESH,
            ).start()

    def near_peer(n):
        ny, nc = near[n]
        return slab_of(ny, z, nc), led

    def far_peer(n):
        return slab_of(y, far[n], core), led

    def finish(semaphores, at, block):
        pltpu.make_async_copy(block, block, semaphores.at[at]).wait()

    with jax.named_scope("wait_load"):
        for load in loads[:5]:
            load.wait()
    row_terms = [term(row_at - led_rows[l]) for l in range(2)]
    pieces = []
    for l in range(2):
        values = []
        masks = [inside(l, block) for block in range(16)]
        for n1 in range(8):
            parts = []
            for part in range(2):
                first = spec[part, :, n1 * 128 : n1 * 128 + 128]
                second = spec[part, :, 1024 + n1 * 128 : 1152 + n1 * 128]
                parts.append(
                    jnp.where(masks[n1], first, 0.0) + jnp.where(masks[n1 + 8], second, 0.0)
                )
            values.append(tuple(parts))
        for k1, (re, im) in enumerate(fft(values, -1)):
            a, b = twist_cols[0, k1 : k1 + 1, :], twist_cols[1, k1 : k1 + 1, :]
            pieces.append(jnp.concatenate([re * a + im * b, im * a - re * b], axis=1))
    result = dot_left(wide, COLS_FWD, jnp.concatenate(pieces, axis=0), 1).astype(BF16)
    for l in range(2):
        send1[:, l * 32 : l * 32 + 32] = result[:, l * 128 : l * 128 + 128].reshape(8, 32, 128)
    recv1[yc] = send1[yc]

    with jax.named_scope("wait_barrier"):
        pl.semaphore_wait(barrier, len(links) + len(near) + len(across))
    greet_links(known)
    exchange(
        len(near),
        lambda n: send1.at[near[n][0] * NC + near[n][1]],
        lambda n: recv1.at[yc],
        near_peer,
        0,
    )

    for load in loads[5:]:
        load.wait()
    moduli = []
    for l in range(2):
        stacked = jnp.concatenate(
            [img[l, :, q * 64 : q * 64 + 64] for q in range(16)], axis=0
        )
        moduli.append(jnp.sqrt(stacked).T)
    moduli = jnp.concatenate(moduli, axis=0)
    tw_re, tw_im = twist_rows[0], twist_rows[1]

    with jax.named_scope("wait_1"):
        finish(got, 0, recv1.at[0:7])
    moved = dot(wide[FOLD], recv1[0:4].reshape(256, 128)) + dot(
        wide[FOLD + 1], recv1[4:8].reshape(256, 128)
    )
    send2[...] = moved.astype(BF16).reshape(16, 16, 128)
    recv2[z] = send2[z]
    with jax.named_scope("wait_known"):
        pl.semaphore_wait(known, len(links))
    exchange(
        len(far), lambda n: send2.at[far[n]], lambda n: recv2.at[z], far_peer, 1
    )

    with jax.named_scope("wait_2"):
        finish(got, 1, recv2.at[0:15])
    strips = recv2[...].reshape(256, 128)
    mixed = dot(wide[ROWS_FWD], strips) + dot(wide[ROWS_FWD + 1], strips)
    rows = []
    for l in range(2):
        re, im = mixed[l * 128 : l * 128 + 64], mixed[l * 128 + 64 : l * 128 + 128]
        rows.append(
            jnp.concatenate([re * tw_re + im * tw_im, im * tw_re - re * tw_im], axis=1)
        )
    field = dot_right(jnp.concatenate(rows, axis=0), wide, SHORT_FWD)
    field_re, field_im = field[:, :128], field[:, 128:]
    factor = moduli / jnp.sqrt(field_re * field_re + field_im * field_im + 0.25) - 1.0
    change = jnp.concatenate([field_re * factor, field_im * factor], axis=1)
    back = dot_right(change, wide, SHORT_INV)
    rows = []
    for l in range(2):
        re, im = back[l * 64 : l * 64 + 64, :128], back[l * 64 : l * 64 + 64, 128:]
        rows.append(re * tw_re - im * tw_im)
        rows.append(im * tw_re + re * tw_im)
    result = dot_left(wide, ROWS_INV, jnp.concatenate(rows, axis=0))
    send3[...] = result.astype(BF16).reshape(64, 4, 128)

    ys = [lax.rem(y + dy, NY) for dy in range(NY)]
    zs = [lax.rem(z + dz, NZ) * NC for dz in range(NZ)]
    cs = [core, NC - 1 - core]
    strips_of = [[lax.rem(y + dy, 2) * (NZ * NC) + zc for zc in zs] for dy in range(2)]
    exchange(
        len(HOPS),
        lambda n: send3.at[strips_of[HOPS[n][0] % 2][HOPS[n][1]] + cs[HOPS[n][2]]],
        lambda n: recv3.at[slab],
        lambda n: (ys[HOPS[n][0]] * (NZ * NC) + zs[HOPS[n][1]] + cs[HOPS[n][2]], led),
        2,
    )
    recv3[slab] = send3[lax.rem(slab, 64)]
    with jax.named_scope("wait_3"):
        finish(got, 2, recv3.at[0:127])

    home = recv3[...].reshape(512, 128)
    spread = dot(cols_inv[0], home) + dot(cols_inv[1], home)
    updates = []
    for l in range(2):
        re = spread[l * 256 : l * 256 + 128].T
        im = spread[l * 256 + 128 : l * 256 + 256].T
        values = []
        for k1 in range(8):
            a, b = twist_cols[0, k1 : k1 + 1, :], twist_cols[1, k1 : k1 + 1, :]
            kr, ki = re[k1 * 16 : k1 * 16 + 16], im[k1 * 16 : k1 * 16 + 16]
            values.append((kr * a - ki * b, ki * a + kr * b))
        updates.append(fft(values, 1))
    for block in range(16):
        masks = [inside(l, block) for l in range(2)]
        for part in range(2):
            total = jnp.where(masks[0], updates[0][block % 8][part], 0.0) + jnp.where(
                masks[1], updates[1][block % 8][part], 0.0
            )
            lanes = slice(block % 4 * 128, block % 4 * 128 + 128)
            grad[block // 4, part, :, lanes] = total
            send5[block // 4, part, :, lanes] = total.astype(BF16)
    exchange(
        len(across),
        lambda n: send5.at[across[n]],
        lambda n: recv5.at[n],
        lambda n: (slab, across[n]),
        3,
    )
    share = out.shape[2]
    total = spec[:, :, pl.ds(pl.multiple_of(led * share, share), share)] + grad[led]
    with jax.named_scope("wait_5"):
        finish(got, 3, recv5)
    for n in range(3):
        total = total + recv5[n].astype(F32)
    out[...] = total
    for at, block in enumerate([send1.at[0:7], send2.at[0:15], recv3.at[0:127], send5.at[0:3]]):
        finish(sent, at, block)


def body(wide, cols_inv, twist_cols, twist_rows, spectrum, led_rows, led_cols, images):
    columns = spectrum.shape[2]
    share = columns // NX
    return pl.pallas_call(
        step_kernel,
        out_shape=pltpu.VMEM((2, 16, share), F32),
        in_specs=[pl.BlockSpec(memory_space=pl.ANY)] * 8,
        out_specs=pl.BlockSpec(memory_space=pltpu.VMEM),
        scratch_shapes=[
            pltpu.SMEM((2,), jnp.int32),
            pltpu.SMEM((2,), jnp.int32),
            pltpu.VMEM((2, 16, columns), F32),
            pltpu.VMEM((2, 8, WIN), F32),
            pltpu.VMEM(wide.shape, BF16),
            pltpu.VMEM(cols_inv.shape, BF16),
            pltpu.VMEM(twist_cols.shape, F32),
            pltpu.VMEM(twist_rows.shape, F32),
            pltpu.VMEM((NX, 2, 16, share), F32),
            pltpu.VMEM((8, 64, 128), BF16),
            pltpu.VMEM((8, 64, 128), BF16),
            pltpu.VMEM((16, 16, 128), BF16),
            pltpu.VMEM((16, 16, 128), BF16),
            pltpu.VMEM((64, 4, 128), BF16),
            pltpu.VMEM((128, 4, 128), BF16),
            pltpu.VMEM((NX, 2, 16, share), BF16),
            pltpu.VMEM((3, 2, 16, share), BF16),
            pltpu.SemaphoreType.DMA((9,)),
            pltpu.SemaphoreType.REGULAR,
            pltpu.SemaphoreType.DMA((4,)),
            pltpu.SemaphoreType.DMA((4,)),
        ],
        compiler_params=pltpu.CompilerParams(collective_id=0, has_side_effects=True),
        name="ptychography_step",
    )(led_rows, led_cols, spectrum, images, wide, cols_inv, twist_cols, twist_rows)


def solution(mesh):
    tables = make_tables()
    placed = (P(None, "slab", None), P("led"), P("led"), P("led", "slab", None))
    mapped = jax.shard_map(
        body,
        mesh=mesh,
        in_specs=(P(),) * 4 + placed,
        out_specs=P(None, "slab", "led"),
        check_vma=False,
    )

    def step(spectrum, led_rows, led_cols, images):
        constants = [jnp.asarray(table) for table in tables]
        return mapped(*constants, spectrum, led_rows, led_cols, images)

    return step
```

time: 46.1 us -> 39.9 us (0.87)
  Pallas kernels: 45.3 us -> 39.2 us
    pallas_call x1, Pallas kernels: 45.3 us -> 39.2 us  [body(): pl.pallas_call(step_kernel, out_shape=pltpu.VMEM((2, 16, share), F32), in...]
where the time goes in v3:
time: 39.9 us; the launch traced here: 39.8 us
  Pallas kernels  39.2 us (98%)
  local copies, waits for them, and re-layouts  0.63 us (2%)
    pallas_call x1, Pallas kernels, body(): pl.pallas_call(step_kernel, out_shape=pltpu.VMEM((2, 16, share), F32), in...  39.2 us

profile of v3, /device:TPU:1, one launch (start us, length us, event | category | flops | bytes accessed | tf_op | source)
XLA Modules:
  0.0 39.8 jit_solution(11560895209609281254)
XLA Ops:
  0.0 39.2 %ptychography_step.1 = f32[2,16,512]{2,1,0:T(8,128)S(1)} custom-call(s32[2]{0:T(128)} %rows_in.1, s32[2]{0:T(128)} %cols_in.1, f32[2,16,2048]{2,1,0:T(8,128)} %spectrum.1, f32[2,8,1024]{2,1,0:T(8,128)} %images.1, bf16[12,256,256]{2,1,0:T(8,128)(2,1)} %constant.8.clone.wide_in, bf16[2,512,512]{2,1,0:T(8,128)(2,1)} %constant.9.clone.cols_inv_in, ...), custom_call_target="tpu_custom_call" | custom-call | tf_op jit(solution)/shard_map/ptychography_step/pallas_call | solution.py:350
  39.2 0.6 %copy.10 = f32[2,16,512]{2,1,0:T(8,128)} copy(f32[2,16,512]{2,1,0:T(8,128)S(1)} %ptychography_step.1) | data formatting | bytes 131072

commit v4 on v3

--- a/solution.py
+++ b/solution.py
@@ -66,10 +66,7 @@
 
 COLS_FWD, SHORT_FWD, SHORT_INV, ROWS_FWD, ROWS_INV, FOLD = range(0, 12, 2)
 LINKS = (1, 3, 4)
-HOPS = sorted(
-    ((dy, dz, dc) for dy in range(NY) for dz in range(NZ) for dc in range(NC)),
-    key=lambda d: -(min(d[0], NY - d[0]) + min(d[1], NZ - d[1]) + 0.1 * d[2]),
-)[:-1]
+FAR_FIRST = (8, 7, 9, 6, 10, 5, 11, 4, 12, 3, 13, 2, 14, 1, 15)
 
 
 def fft(values, sign):
@@ -129,14 +126,15 @@
     z = lax.rem(lax.div(slab, NC), NZ)
     y = lax.div(slab, NC * NZ)
     yc = y * NC + core
+    idle_y = jnp.where(z < NZ // 2, 0, NY - 1)
+    idle = y == idle_y
 
     def slab_of(ny, nz, nc):
         return (ny * NZ + nz) * NC + nc
 
     near = [(2, 1), (2, 0), (1, 1), (3, 1), (1, 0), (3, 0), (0, 1)]
     near = [(lax.rem(y + dy, NY), lax.rem(core + dc, NC)) for dy, dc in near]
-    far = [8, 7, 9, 6, 10, 5, 11, 4, 12, 3, 13, 2, 14, 1, 15]
-    far = [lax.rem(z + dz, NZ) for dz in far]
+    far = [lax.rem(z + dz, NZ) for dz in FAR_FIRST]
     across = [lax.rem(led + dx, NX) for dx in (2, 1, 3)]
 
     loads = [
@@ -231,17 +229,26 @@
     for l in range(2):
         send1[:, l * 32 : l * 32 + 32] = result[:, l * 128 : l * 128 + 128].reshape(8, 32, 128)
     recv1[yc] = send1[yc]
+    for nc in range(NC):
+        recv1[idle_y * NC + nc] = jnp.zeros_like(recv1[0])
+
+    @pl.when(idle)
+    def _():
+        recv3[...] = jnp.zeros_like(recv3)
 
     with jax.named_scope("wait_barrier"):
         pl.semaphore_wait(barrier, len(links) + len(near) + len(across))
     greet_links(known)
-    exchange(
-        len(near),
-        lambda n: send1.at[near[n][0] * NC + near[n][1]],
-        lambda n: recv1.at[yc],
-        near_peer,
-        0,
-    )
+
+    @pl.when(jnp.logical_not(idle))
+    def _():
+        exchange(
+            len(near),
+            lambda n: send1.at[near[n][0] * NC + near[n][1]],
+            lambda n: recv1.at[yc],
+            near_peer,
+            0,
+        )
 
     for load in loads[5:]:
         load.wait()
@@ -255,7 +262,15 @@
     tw_re, tw_im = twist_rows[0], twist_rows[1]
 
     with jax.named_scope("wait_1"):
-        finish(got, 0, recv1.at[0:7])
+
+        @pl.when(jnp.logical_not(idle))
+        def _():
+            finish(got, 0, recv1.at[0:5])
+
+        @pl.when(idle)
+        def _():
+            finish(got, 0, recv1.at[0:6])
+
     moved = dot(wide[FOLD], recv1[0:4].reshape(256, 128)) + dot(
         wide[FOLD + 1], recv1[4:8].reshape(256, 128)
     )
@@ -281,29 +296,47 @@
     field_re, field_im = field[:, :128], field[:, 128:]
     factor = moduli / jnp.sqrt(field_re * field_re + field_im * field_im + 0.25) - 1.0
     change = jnp.concatenate([field_re * factor, field_im * factor], axis=1)
-    back = dot_right(change, wide, SHORT_INV)
+    change = change.astype(BF16)
+    back = dot(change, wide[SHORT_INV]) + dot(change, wide[SHORT_INV + 1])
     rows = []
     for l in range(2):
         re, im = back[l * 64 : l * 64 + 64, :128], back[l * 64 : l * 64 + 64, 128:]
         rows.append(re * tw_re - im * tw_im)
         rows.append(im * tw_re + re * tw_im)
-    result = dot_left(wide, ROWS_INV, jnp.concatenate(rows, axis=0))
+    rows = jnp.concatenate(rows, axis=0).astype(BF16)
+    result = dot(wide[ROWS_INV], rows) + dot(wide[ROWS_INV + 1], rows)
     send3[...] = result.astype(BF16).reshape(64, 4, 128)
 
-    ys = [lax.rem(y + dy, NY) for dy in range(NY)]
-    zs = [lax.rem(z + dz, NZ) * NC for dz in range(NZ)]
-    cs = [core, NC - 1 - core]
-    strips_of = [[lax.rem(y + dy, 2) * (NZ * NC) + zc for zc in zs] for dy in range(2)]
-    exchange(
-        len(HOPS),
-        lambda n: send3.at[strips_of[HOPS[n][0] % 2][HOPS[n][1]] + cs[HOPS[n][2]]],
-        lambda n: recv3.at[slab],
-        lambda n: (ys[HOPS[n][0]] * (NZ * NC) + zs[HOPS[n][1]] + cs[HOPS[n][2]], led),
-        2,
-    )
-    recv3[slab] = send3[lax.rem(slab, 64)]
+    def send_back(ny, nz, nc):
+        pltpu.make_async_remote_copy(
+            src_ref=send3.at[(lax.rem(ny, 2) * NZ + nz) * NC + nc],
+            dst_ref=recv3.at[slab],
+            send_sem=sent.at[2],
+            recv_sem=got.at[2],
+            device_id=(slab_of(ny, nz, nc), led),
+            device_id_type=MESH,
+        ).start()
+
+    for dz in FAR_FIRST + (0,):
+        nz = lax.rem(z + dz, NZ)
+        edge = jnp.where(nz < NZ // 2, NY - 1, 0)
+        for nc in (NC - 1 - core, core):
+            for ny in (edge, 1, 2):
+                if dz == 0 and nc is core:
+                    pl.when(y != ny)(functools.partial(send_back, ny, nz, nc))
+                else:
+                    send_back(ny, nz, nc)
+
+    @pl.when(jnp.logical_not(idle))
+    def _():
+        recv3[slab] = send3[lax.rem(slab, 64)]
+
     with jax.named_scope("wait_3"):
-        finish(got, 2, recv3.at[0:127])
+
+        @pl.when(jnp.logical_not(idle))
+        def _():
+            finish(got, 2, recv3.at[0:127])
+
 
     home = recv3[...].reshape(512, 128)
     spread = dot(cols_inv[0], home) + dot(cols_inv[1], home)
@@ -340,8 +373,17 @@
     for n in range(3):
         total = total + recv5[n].astype(F32)
     out[...] = total
-    for at, block in enumerate([send1.at[0:7], send2.at[0:15], recv3.at[0:127], send5.at[0:3]]):
+    for at, block in ((1, send2.at[0:15]), (3, send5.at[0:3])):
         finish(sent, at, block)
+
+    @pl.when(idle)
+    def _():
+        finish(sent, 2, recv3.at[0:96])
+
+    @pl.when(jnp.logical_not(idle))
+    def _():
+        finish(sent, 0, send1.at[0:7])
+        finish(sent, 2, recv3.at[0:95])
 
 
 def body(wide, cols_inv, twist_cols, twist_rows, spectrum, led_rows, led_cols, images):

time: 39.9 us -> 38.6 us (0.967)
  the two profiles are of different devices: /device:TPU:1 before, /device:TPU:8 now
where the time goes in v4:
time: 38.6 us; the launch traced here: 38.5 us
  Pallas kernels  37.8 us (98%)
  local copies, waits for them, and re-layouts  0.63 us (2%)
    pallas_call x1, Pallas kernels, body(): pl.pallas_call(step_kernel, out_shape=pltpu.VMEM((2, 16, share), F32), in...  37.8 us

profile of v4, /device:TPU:8, one launch (start us, length us, event | category | flops | bytes accessed | tf_op | source)
XLA Modules:
  0.0 38.5 jit_solution(18068666106061561196)
XLA Ops:
  0.0 37.8 %ptychography_step.1 = f32[2,16,512]{2,1,0:T(8,128)S(1)} custom-call(s32[2]{0:T(128)} %rows_in.1, s32[2]{0:T(128)} %cols_in.1, f32[2,16,2048]{2,1,0:T(8,128)} %spectrum.1, f32[2,8,1024]{2,1,0:T(8,128)} %images.1, bf16[12,256,256]{2,1,0:T(8,128)(2,1)} %constant.8.clone.wide_in, bf16[2,512,512]{2,1,0:T(8,128)(2,1)} %constant.9.clone.cols_inv_in, ...), custom_call_target="tpu_custom_call" | custom-call | tf_op jit(solution)/shard_map/ptychography_step/pallas_call | solution.py:392
  37.8 0.6 %copy.10 = f32[2,16,512]{2,1,0:T(8,128)} copy(f32[2,16,512]{2,1,0:T(8,128)S(1)} %ptychography_step.1) | data formatting | bytes 131072

commit v5 on v4

--- a/solution.py
+++ b/solution.py
@@ -61,7 +61,7 @@
     p, k1, i = grid_of(64, 8, 16)
     angle = (2.0 * np.pi * ((p * i) % WIN) / WIN).reshape(64, 128)
     twist_rows = np.stack([np.cos(angle), np.sin(angle)]).astype(np.float32)
-    return np.stack(wide), np.stack(split(cols_inv)), twist_cols, twist_rows
+    return np.stack(wide), split(cols_inv)[0], twist_cols, twist_rows
 
 
 COLS_FWD, SHORT_FWD, SHORT_INV, ROWS_FWD, ROWS_INV, FOLD = range(0, 12, 2)
@@ -110,11 +110,6 @@
     )
 
 
-def dot_right(value, tables, at):
-    high, low = halves(value)
-    return dot(high, tables[at]) + dot(low, tables[at]) + dot(high, tables[at + 1])
-
-
 def step_kernel(
     rows_in, cols_in, spectrum, images, wide_in, cols_inv_in, twist_cols_in, twist_rows_in, out,
     led_rows, led_cols, spec, img, wide, cols_inv, twist_cols, twist_rows, grad,
@@ -153,8 +148,6 @@
             ]
         )
     ]
-    for load in loads[:5]:
-        load.start()
     barrier = pltpu.get_barrier_semaphore()
 
     links = [lax.rem(z + dz, NZ) for d in LINKS for dz in (d, NZ - d)]
@@ -172,7 +165,7 @@
         )
     for nx in across:
         pl.semaphore_signal(barrier, inc=1, device_id=(slab, nx), device_id_type=MESH)
-    for load in loads[5:]:
+    for load in loads:
         load.start()
 
     row_at = slab * 16 + lax.broadcasted_iota(jnp.int32, (16, 128), 0)
@@ -292,7 +285,8 @@
         rows.append(
             jnp.concatenate([re * tw_re + im * tw_im, im * tw_re - re * tw_im], axis=1)
         )
-    field = dot_right(jnp.concatenate(rows, axis=0), wide, SHORT_FWD)
+    rows = jnp.concatenate(rows, axis=0).astype(BF16)
+    field = dot(rows, wide[SHORT_FWD]) + dot(rows, wide[SHORT_FWD + 1])
     field_re, field_im = field[:, :128], field[:, 128:]
     factor = moduli / jnp.sqrt(field_re * field_re + field_im * field_im + 0.25) - 1.0
     change = jnp.concatenate([field_re * factor, field_im * factor], axis=1)
@@ -339,7 +333,7 @@
 
 
     home = recv3[...].reshape(512, 128)
-    spread = dot(cols_inv[0], home) + dot(cols_inv[1], home)
+    spread = dot(cols_inv[...], home)
     updates = []
     for l in range(2):
         re = spread[l * 256 : l * 256 + 128].T

time: 38.6 us -> 38.5 us (level)
  no operation moved by 1% of the time
where the time goes in v5:
time: 38.5 us; the launch traced here: 38.4 us
  Pallas kernels  37.7 us (98%)
  local copies, waits for them, and re-layouts  0.63 us (2%)
    pallas_call x1, Pallas kernels, body(): pl.pallas_call(step_kernel, out_shape=pltpu.VMEM((2, 16, share), F32), in...  37.7 us

profile of v5, /device:TPU:8, one launch (start us, length us, event | category | flops | bytes accessed | tf_op | source)
XLA Modules:
  0.0 38.4 jit_solution(1156430991185297842)
XLA Ops:
  0.0 37.7 %ptychography_step.1 = f32[2,16,512]{2,1,0:T(8,128)S(1)} custom-call(s32[2]{0:T(128)} %rows_in.1, s32[2]{0:T(128)} %cols_in.1, f32[2,16,2048]{2,1,0:T(8,128)} %spectrum.1, f32[2,8,1024]{2,1,0:T(8,128)} %images.1, bf16[12,256,256]{2,1,0:T(8,128)(2,1)} %constant.8.clone.wide_in, bf16[512,512]{1,0:T(8,128)(2,1)} %constant.9.clone.cols_inv_in, ...), custom_call_target="tpu_custom_call" | custom-call | tf_op jit(solution)/shard_map/ptychography_step/pallas_call | solution.py:386
  37.7 0.6 %copy.10 = f32[2,16,512]{2,1,0:T(8,128)} copy(f32[2,16,512]{2,1,0:T(8,128)S(1)} %ptychography_step.1) | data formatting | bytes 131072
